TPU v7x, 256 devices: a whole 4x4x8 slice. The times are simulated.
256 devices in a mesh: group: 8 (over x_lo, y), member: 32 (over x_hi, z, core).
Axes of the slice: x: 4 (x_hi: 2, x_lo: 2; x = x_hi * 2 + x_lo), y: 4, z: 8, core: 2. Of those that a mesh axis runs over, the one named last changes fastest.
Arguments:
- entity: bfloat16 [65536, 800], P(('group', 'member')), may hold values from -3 to 7.5
- adagrad_state: float32 [65536], P(('group', 'member')), may hold values from 0.01 to 1
- relation: bfloat16 [1345, 800], replicated, may hold values from -1.8 to 1.8
- source_ids: int32 [2, 131072], P(None, ('group', 'member')), may hold values from 0 to 255
- relation_ids: int32 [2, 131072], P(None, ('group', 'member')), may hold values from 0 to 1344
- dest_groups: int32 [2, 131072, 1], P(None, ('group', 'member')), may hold values from 0 to 7; in each aligned block of 512 rows (0 to 511, 512 to 1023, ..., all dimensions but the last counted through in order) at most 128 rows name the same one
- dest_rows: int32 [2, 131072], P(None, ('group', 'member')), may hold values from 0 to 255
- negative_ids: int32 [2, 256000], P(None, ('group', 'member')), may hold values from 0 to 255
- owners: int32 [2, 8], replicated, may hold values from 0 to 31
Outputs:
- new_entity: bfloat16 [65536, 800], P(('group', 'member'))
- new_state: float32 [65536], P(('group', 'member'))
Inputs may be any that keep to these rules, and one draw needn't show every extreme that they name: `dest_groups`: for each sub-step and each device's 512 edges, at most 128 name any one destination group, a bound that some block reaches.
All inputs are finite; a program needn't handle non-finite values.
Results may differ from a plain program's by a relative error of at most 0.017.
Values may be sent and summed in bfloat16 or wider, within the bound.
A program may use at most 64 MiB of HBM per device.

v0:
```python
import jax
import jax.numpy as jnp
from jax import lax
from jax.sharding import PartitionSpec as P


def broadcast(value, axis, source):
    kept = jnp.where(lax.axis_index(axis) == source, value, 0).astype(value.dtype)
    return lax.psum(kept, axis)


def complex_query(source, rel):
    half = source.shape[-1] // 2
    sr, si = (source[..., :half], source[..., half:])
    rr, ri = (rel[..., :half], rel[..., half:])
    return jnp.concatenate([sr * rr - si * ri, sr * ri + si * rr], -1)


def source_grad(grad_query, rel):
    half = grad_query.shape[-1] // 2
    gr, gi = (grad_query[..., :half], grad_query[..., half:])
    rr, ri = (rel[..., :half], rel[..., half:])
    return jnp.concatenate([gr * rr + gi * ri, gi * rr - gr * ri], -1)


def edge_terms(source_rows, rel_rows, dest_rows, negatives):
    rel = rel_rows.astype(jnp.float32)
    query = complex_query(source_rows.astype(jnp.float32), rel).astype(jnp.bfloat16)
    dest = dest_rows.astype(jnp.float32)
    positive = jnp.sum(query.astype(jnp.float32) * dest, -1)
    scores = lax.dot_general(
        query, negatives, (((1,), (1,)), ((), ())), preferred_element_type=jnp.float32
    )
    top = jnp.maximum(jnp.max(scores, 1), positive)
    pos_exp = jnp.exp(positive - top)
    neg_exp = jnp.exp(scores - top[:, None])
    total = pos_exp + jnp.sum(neg_exp, 1)
    coef_pos = pos_exp / total - 1.0
    coef_neg = (neg_exp / total[:, None]).astype(jnp.bfloat16)
    grad_query = coef_pos[:, None] * dest + jnp.dot(
        coef_neg, negatives, preferred_element_type=jnp.float32
    )
    grad_source = source_grad(grad_query, rel)
    grad_neg = lax.dot_general(
        coef_neg, query, (((0,), (0,)), ((), ())), preferred_element_type=jnp.float32
    )
    return (grad_source, query, coef_pos, grad_neg)


def scatter_rows(values, row_ids, count):
    onehot = (row_ids[:, None] == jnp.arange(count, dtype=jnp.int32)[None, :]).astype(jnp.float32)
    return lax.dot_general(
        onehot,
        values,
        (((0,), (0,)), ((), ())),
        precision=lax.Precision.HIGHEST,
        preferred_element_type=jnp.float32,
    )


def per_device(
    entity,
    adagrad_state,
    relation,
    source_ids,
    relation_ids,
    dest_groups,
    dest_rows,
    negative_ids,
    owners,
):
    groups = lax.axis_size("group")
    group_index = lax.axis_index("group")
    member_index = lax.axis_index("member")
    shard_rows = entity.shape[0]
    table = entity
    state = adagrad_state
    for step in range(source_ids.shape[0]):
        root = owners[step, group_index]
        block = broadcast(table, "member", root)
        src = source_ids[step]
        rel = relation_ids[step]
        dgr = dest_groups[step, :, 0]
        drw = dest_rows[step]
        neg = negative_ids[step]
        source_rows = jnp.take(block, src, axis=0)
        rel_rows = jnp.take(relation, rel, axis=0)
        negatives = jnp.take(table, neg, axis=0)
        whole = lax.all_gather(table, "group", axis=0, tiled=True)
        flat = dgr * shard_rows + drw
        dest_vals = jnp.take(whole, flat, axis=0)
        grad_source, query, coef_pos, grad_neg = edge_terms(
            source_rows, rel_rows, dest_vals, negatives
        )
        grad_dest = coef_pos[:, None] * query.astype(jnp.float32)
        spread = scatter_rows(grad_dest, flat, groups * shard_rows)
        dest_total = lax.psum_scatter(spread, "group", scatter_dimension=0, tiled=True)
        source_part = scatter_rows(grad_source, src, shard_rows)
        source_total = lax.psum(source_part, "member")
        neg_total = scatter_rows(grad_neg, neg, shard_rows)
        grads = dest_total + neg_total + jnp.where(member_index == root, source_total, 0.0)
        state = state + jnp.mean(grads * grads, -1)
        table = (table.astype(jnp.float32) - 1.0 * grads / jnp.sqrt(state)[:, None]).astype(
            jnp.bfloat16
        )
    return (table, state)


def solution(mesh):
    placed = (
        P(("group", "member"), None),
        P(("group", "member")),
        P(),
        P(None, ("group", "member")),
        P(None, ("group", "member")),
        P(None, ("group", "member"), None),
        P(None, ("group", "member")),
        P(None, ("group", "member")),
        P(),
    )
    return jax.shard_map(
        per_device,
        mesh=mesh,
        in_specs=placed,
        out_specs=(P(("group", "member"), None), P(("group", "member"))),
        check_vma=False,
    )
```

profile of v0, /device:TPU:16, one launch (start us, length us, event | category | flops | bytes accessed | tf_op | source)
XLA Modules:
  0.0 1122.0 jit_solution(834115604931892025)
XLA Ops:
  14.0 5.3 gather_fusion.3
  19.3 3.4 copy.13
  22.8 2.1 gather_fusion.1
  26.3 246.0 %all-reduce.5.cloned.1.call-done = bf16[256,800]{0,1:T(8,128)(2,1)} async-done(((bf16[256,800]{0,1:T(8,128)(2,1)}), bf16[256,800]{0,1:T(8,128)(2,1)}) %all-reduce.5.cloned.1.call-update) | async-done | bytes 409616 | tf_op jit(solution)/shard_map/psum | solution.py:9
  273.5 2.8 gather_fusion
  276.3 2.3 copy.12
  282.0 2.6 fusion.44
  284.5 5.0 gather_fusion.2
  294.7 3.0 fusion.7
  300.2 7.7 fusion
  308.7 4.7 fusion.38
  313.4 244.1 %all-reduce.7.cloned.1.call-done = f32[256,800]{0,1:T(8,128)} async-done(((f32[256,800]{0,1:T(8,128)}), f32[256,800]{0,1:T(8,128)}) %all-reduce.7.cloned.1.call-update) | async-done | bytes 819216 | tf_op jit(solution)/shard_map/psum | solution.py:99
  557.5 5.4 multiply_reduce_fusion.1
  564.9 2.1 gather_fusion.5
  569.9 5.3 gather_fusion.7
  575.2 243.6 %all-reduce.9.cloned.1.call-done = bf16[256,800]{0,1:T(8,128)(2,1)} async-done(((bf16[256,800]{0,1:T(8,128)(2,1)}), bf16[256,800]{0,1:T(8,128)(2,1)}) %all-reduce.9.cloned.1.call-update) | async-done | bytes 409616 | tf_op jit(solution)/shard_map/psum | solution.py:9
  826.2 2.6 fusion.45
  828.9 6.0 copy.22
  834.9 5.0 gather_fusion.6
  844.9 2.9 fusion.9
  850.4 7.7 fusion.1
  859.7 3.1 fusion.37
  862.8 244.7 %all-reduce.11.cloned.1.call-done = f32[256,800]{0,1:T(8,128)} async-done(((f32[256,800]{0,1:T(8,128)}), f32[256,800]{0,1:T(8,128)}) %all-reduce.11.cloned.1.call-update) | async-done | bytes 819216 | tf_op jit(solution)/shard_map/psum | solution.py:99
  1107.5 5.7 multiply_reduce_fusion
  (132 shorter events, 41.8 us)
Async XLA Ops:
  8.0 5.1 copy-start.19
  8.0 264.3 %all-reduce.5.cloned.1.call-start = ((), (), s32[]{:S(2)}) async-start(), calls=%async_computation.2 | async-start | bytes 819200 | tf_op jit(solution)/shard_map/psum | solution.py:9
  10.9 273.6 %all-gather.3.cloned.1.call-start = ((), (), s32[]{:S(2)}) async-start(), calls=%async_computation.3 | async-start | bytes 4128768 | tf_op jit(solution)/shard_map/all_gather | solution.py:89
  13.0 544.4 %all-reduce.7.cloned.1.call-start = ((), (), s32[]{:S(2)}) async-start(), calls=%async_computation.5 | async-start | bytes 1638400 | tf_op jit(solution)/shard_map/psum | solution.py:99
  19.3 3.4 copy-start.21
  22.8 3.4 copy-start.22
  22.8 3.4 copy-start.23
  22.8 3.4 copy-start.24
  276.3 2.3 copy-start.7
  290.9 3.8 copy-start.5
  290.9 3.8 copy-start.8
  294.6 3.0 copy-start.2
  300.0 257.5 %reduce-scatter.3.cloned.1.call-start = ((), (), s32[]{:S(2)}) async-start(), calls=%async_computation.4 | async-start | bytes 7372800 | tf_op jit(solution)/shard_map/reduce_scatter | solution.py:97
  308.0 510.8 %all-reduce.9.cloned.1.call-start = ((), (), s32[]{:S(2)}) async-start(), calls=%async_computation.6 | async-start | bytes 819200 | tf_op jit(solution)/shard_map/psum | solution.py:9
  313.3 249.6 %copy-start.20 = (f32[256]{0:T(256)S(1)}, f32[256]{0:T(256)}, u32[]{:S(2)}) copy-start(f32[256]{0:T(256)} %param.18) | copy-start | bytes 3076
  313.3 249.6 %copy-start.4 = (bf16[256,800]{0,1:T(8,128)(2,1)S(1)}, bf16[256,800]{0,1:T(8,128)(2,1)}, u32[]{:S(2)}) copy-start(bf16[256,800]{0,1:T(8,128)(2,1)} %param.17) | copy-start | bytes 1228804
  564.0 264.8 %all-gather.5.cloned.1.call-start = ((), (), s32[]{:S(2)}) async-start(), calls=%async_computation.7 | async-start | bytes 3686400 | tf_op jit(solution)/shard_map/all_gather | solution.py:89
  564.6 542.9 %all-reduce.11.cloned.1.call-start = ((), (), s32[]{:S(2)}) async-start(), calls=%async_computation.9 | async-start | bytes 1638400 | tf_op jit(solution)/shard_map/psum | solution.py:99
  567.0 2.7 copy-start.3
  825.1 3.8 copy-start.17
  841.2 3.7 copy-start.6
  841.2 3.7 copy-start.9
  848.1 2.3 copy-start.18
  850.1 257.5 %reduce-scatter.5.cloned.1.call-start = ((), (), s32[]{:S(2)}) async-start(), calls=%async_computation.8 | async-start | bytes 7372800 | tf_op jit(solution)/shard_map/reduce_scatter | solution.py:97
  (9 other events, 13.6 us)
Sparse Core Ops, SparseCore 0:
  12.0 260.1 all-reduce.4
  300.1 257.3 all-reduce.6
  564.2 254.5 all-reduce.8
  850.2 257.2 all-reduce.10
Sparse Core Ops, SparseCore 1:
  13.3 51.3 all-gather.2
  308.1 72.5 reduce-scatter.2
  566.3 53.8 all-gather.4
  858.2 72.5 reduce-scatter.4
where the time goes:
time: 1120 us
  waiting for transfers between devices  979 us (87%)
  local copies, waits for them, and re-layouts  59 us (5%)
  matrix products  49.2 us (4%)
  between operations  17.3 us (2%)
  other arithmetic  16.4 us (1%)
    psum x2, waiting for transfers between devices, broadcast(): return lax.psum(kept, axis)  490 us
    psum x2, waiting for transfers between devices, per_device(): source_total = lax.psum(source_part, 'member')  489 us
    dot_general x6, matrix products, scatter_rows(): lax.dot_general(onehot, values, (((0,), (0,)), ((), ())), precision=lax.P...  30.4 us
  transfers between devices with their start and end apart: 8, of which 4 were waited for; matrix products, arithmetic and copies ran while one was open for 6% of the time, Pallas kernels for 0%

commit v1 on v0

--- a/solution.py
+++ b/solution.py
@@ -6,7 +6,7 @@
 
 def broadcast(value, axis, source):
     kept = jnp.where(lax.axis_index(axis) == source, value, 0).astype(value.dtype)
-    return lax.psum(kept, axis)
+    return jnp.sum(lax.all_gather(kept, axis), axis=0)
 
 
 def complex_query(source, rel):

time: 1120 us -> 1160 us (1.036); the launches traced: 1120 us -> 1150 us
  local copies, waits for them, and re-layouts: 59 us -> 80.5 us
  other arithmetic: 16.4 us -> 31.9 us
    psum x2 -> x0, waiting for transfers between devices: 490 us -> none  [broadcast(): return lax.psum(kept, axis)]
    all_gather x0 -> x2, waiting for transfers between devices: none -> 255 us  [broadcast(): return jnp.sum(lax.all_gather(kept, axis), axis=0)]
    reduce_scatter x2, waiting for transfers between devices: 0.01 us -> 151 us  [per_device(): lax.psum_scatter(spread, 'group', scatter_dimension=0, tiled=True)]
    all_gather x2, waiting for transfers between devices: 0.01 us -> 82.1 us  [per_device(): whole = lax.all_gather(table, 'group', axis=0, tiled=True)]
    unnamed x52 -> x38, local copies, waits for them, and re-layouts: 10.7 us -> 33.8 us
    reduce_sum x0 -> x2, other arithmetic: none -> 21.5 us  [broadcast(): return jnp.sum(lax.all_gather(kept, axis), axis=0)]
  transfers between devices with their start and end apart: 8 -> 8, of which waited for: 4 -> 8; matrix products, arithmetic and copies ran while one was open for 6% -> 6% of each run, Pallas kernels for 0% -> 0%
where the time goes in v1:
time: 1160 us; the launch traced here: 1150 us
  waiting for transfers between devices  973 us (84%)
  local copies, waits for them, and re-layouts  80.5 us (7%)
  matrix products  43.7 us (4%)
  other arithmetic  31.9 us (3%)
  between operations  16.4 us (1%)
    psum x2, waiting for transfers between devices, per_device(): source_total = lax.psum(source_part, 'member')  485 us
    all_gather x2, waiting for transfers between devices, broadcast(): return jnp.sum(lax.all_gather(kept, axis), axis=0)  255 us
    reduce_scatter x2, waiting for transfers between devices, per_device(): lax.psum_scatter(spread, 'group', scatter_dimension=0, tiled=True)  151 us
    all_gather x2, waiting for transfers between devices, per_device(): whole = lax.all_gather(table, 'group', axis=0, tiled=True)  82.1 us
    unnamed x38, local copies, waits for them, and re-layouts  33.8 us
    dot_general x6, matrix products, scatter_rows(): lax.dot_general(onehot, values, (((0,), (0,)), ((), ())), precision=lax.P...  30.6 us
  transfers between devices with their start and end apart: 8, of which 8 were waited for; matrix products, arithmetic and copies ran while one was open for 6% of the time, Pallas kernels for 0%

profile of v1, /device:TPU:16, one launch (start us, length us, event | category | flops | bytes accessed | tf_op | source)
XLA Modules:
  0.0 1146.4 jit_solution(9447415240493280149)
XLA Ops:
  12.3 5.3 gather_fusion.3
  17.5 3.4 copy.25
  24.5 36.0 %all-gather.7.cloned.1.call-done = bf16[2048,800]{1,0:T(8,128)(2,1)} async-done(((bf16[256,800]{1,0:T(8,128)(2,1)}), bf16[2048,800]{1,0:T(8,128)(2,1)}) %all-gather.7.cloned.1.call-update) | async-done | bytes 3276816 | tf_op jit(solution)/shard_map/all_gather | solution.py:89
  60.5 5.0 gather_fusion.2
  66.8 131.0 %all-gather.11.cloned.1.call-done = bf16[8192,800]{0,1:T(8,128)(2,1)} async-done(((bf16[256,800]{0,1:T(8,128)(2,1)}), bf16[8192,800]{0,1:T(8,128)(2,1)}) %all-gather.11.cloned.1.call-update) | async-done | bytes 13107216 | tf_op jit(solution)/shard_map/all_gather | solution.py:9
  197.8 12.5 %copy.37 = bf16[100,8,32,256]{3,2,1,0:T(8,128)(2,1)} copy(bf16[100,8,32,256]{3,1,2,0:T(8,128)(2,1)} %bitcast.24) | data formatting | bytes 26214400
  210.2 10.8 bitcast_reduce_fusion.1
  235.1 7.7 fusion
  243.5 4.7 fusion.38
  248.2 242.1 %all-reduce.3.cloned.1.call-done = f32[256,800]{0,1:T(8,128)} async-done(((f32[256,800]{0,1:T(8,128)}), f32[256,800]{0,1:T(8,128)}) %all-reduce.3.cloned.1.call-update) | async-done | bytes 819216 | tf_op jit(solution)/shard_map/psum | solution.py:99
  490.4 75.4 %reduce-scatter.3.cloned.1.call-done = f32[256,800]{0,1:T(8,128)} async-done(((f32[2048,800]{0,1:T(8,128)}), f32[256,800]{0,1:T(8,128)}) %reduce-scatter.3.cloned.1.call-update) | async-done | bytes 819216 | tf_op jit(solution)/shard_map/reduce_scatter | solution.py:97
  565.7 5.4 multiply_reduce_fusion.1
  578.1 5.3 gather_fusion.7
  583.4 46.1 %all-gather.9.cloned.1.call-done = bf16[2048,800]{0,1:T(8,128)(2,1)} async-done(((bf16[256,800]{0,1:T(8,128)(2,1)}), bf16[2048,800]{0,1:T(8,128)(2,1)}) %all-gather.9.cloned.1.call-update) | async-done | bytes 3276816 | tf_op jit(solution)/shard_map/all_gather | solution.py:89
  629.4 6.0 copy.34
  635.4 5.0 gather_fusion.6
  641.7 124.3 %all-gather.13.cloned.1.call-done = bf16[8192,800]{0,1:T(8,128)(2,1)} async-done(((bf16[256,800]{0,1:T(8,128)(2,1)}), bf16[8192,800]{0,1:T(8,128)(2,1)}) %all-gather.13.cloned.1.call-update) | async-done | bytes 13107216 | tf_op jit(solution)/shard_map/all_gather | solution.py:9
  766.0 12.5 %copy.38 = bf16[100,8,32,256]{3,2,1,0:T(8,128)(2,1)} copy(bf16[100,8,32,256]{3,1,2,0:T(8,128)(2,1)} %bitcast.25) | data formatting | bytes 26214400
  778.5 10.8 bitcast_reduce_fusion
  801.5 8.0 fusion.1
  811.0 3.1 fusion.37
  814.1 242.6 %all-reduce.5.cloned.1.call-done = f32[256,800]{0,1:T(8,128)} async-done(((f32[256,800]{0,1:T(8,128)}), f32[256,800]{0,1:T(8,128)}) %all-reduce.5.cloned.1.call-update) | async-done | bytes 819216 | tf_op jit(solution)/shard_map/psum | solution.py:99
  1056.7 75.3 %reduce-scatter.5.cloned.1.call-done = f32[256,800]{0,1:T(8,128)} async-done(((f32[2048,800]{0,1:T(8,128)}), f32[256,800]{0,1:T(8,128)}) %reduce-scatter.5.cloned.1.call-update) | async-done | bytes 819216 | tf_op jit(solution)/shard_map/reduce_scatter | solution.py:97
  1132.0 5.7 multiply_reduce_fusion
  (120 shorter events, 46.3 us)
Async XLA Ops:
  7.2 5.0 copy-start.11
  7.2 53.3 %all-gather.7.cloned.1.call-start = ((), (), s32[]{:S(2)}) async-start(), calls=%async_computation.2 | async-start | bytes 4128768 | tf_op jit(solution)/shard_map/all_gather | solution.py:89
  9.2 3.1 copy-start
  9.2 188.5 %all-gather.11.cloned.1.call-start = ((), (), s32[]{:S(2)}) async-start(), calls=%async_computation.8 | async-start | bytes 13516800 | tf_op jit(solution)/shard_map/all_gather | solution.py:9
  12.2 478.2 %all-reduce.3.cloned.1.call-start = ((), (), s32[]{:S(2)}) async-start(), calls=%async_computation.4 | async-start | bytes 1638400 | tf_op jit(solution)/shard_map/psum | solution.py:99
  17.5 3.4 copy-start.13
  21.0 3.3 copy-start.14
  21.0 3.4 copy-start.15
  21.0 3.4 copy-start.16
  224.3 2.3 copy-start.5
  227.9 1.1 copy-start.3
  228.0 1.7 copy-start.9
  231.0 1.8 copy-start.6
  235.1 330.7 %reduce-scatter.3.cloned.1.call-start = ((), (), s32[]{:S(2)}) async-start(), calls=%async_computation.3 | async-start | bytes 7372800 | tf_op jit(solution)/shard_map/reduce_scatter | solution.py:97
  242.9 386.6 %all-gather.9.cloned.1.call-start = ((), (), s32[]{:S(2)}) async-start(), calls=%async_computation.5 | async-start | bytes 3686400 | tf_op jit(solution)/shard_map/all_gather | solution.py:89
  248.2 322.9 %copy-start.12 = (f32[256]{0:T(256)S(1)}, f32[256]{0:T(256)}, u32[]{:S(2)}) copy-start(f32[256]{0:T(256)} %param.18) | copy-start | bytes 3076
  248.2 323.0 %copy-start.2 = (bf16[256,800]{0,1:T(8,128)(2,1)S(1)}, bf16[256,800]{0,1:T(8,128)(2,1)}, u32[]{:S(2)}) copy-start(bf16[256,800]{0,1:T(8,128)(2,1)} %param.17) | copy-start | bytes 1228804
  572.3 193.7 %all-gather.13.cloned.1.call-start = ((), (), s32[]{:S(2)}) async-start(), calls=%async_computation.9 | async-start | bytes 13516800 | tf_op jit(solution)/shard_map/all_gather | solution.py:9
  572.9 483.8 %all-reduce.5.cloned.1.call-start = ((), (), s32[]{:S(2)}) async-start(), calls=%async_computation.7 | async-start | bytes 1638400 | tf_op jit(solution)/shard_map/psum | solution.py:99
  575.2 2.6 copy-start.1
  794.3 1.7 copy-start.10
  797.3 1.8 copy-start.7
  801.4 330.6 %reduce-scatter.5.cloned.1.call-start = ((), (), s32[]{:S(2)}) async-start(), calls=%async_computation.6 | async-start | bytes 7372800 | tf_op jit(solution)/shard_map/reduce_scatter | solution.py:97
  809.4 1.6 copy-start.8
  (1 other events, 1.1 us)
Sparse Core Ops, SparseCore 0:
  9.8 50.6 all-gather.6
  63.6 134.0 all-gather.10
  235.2 255.1 all-reduce.2
  493.0 72.7 reduce-scatter.2
  572.4 56.9 all-gather.8
  632.8 133.2 all-gather.12
  801.5 255.1 all-reduce.4
  1059.3 72.6 reduce-scatter.4
